TPU v7x, 32 devices: a whole 2x2x4 slice. The times are simulated.
32 devices in a mesh: groups: 2 (over y), tile: 4 (over z), chan: 4 (over x, core).
Axes of the slice: x: 2, y: 2, z: 4, core: 2. Of those that a mesh axis runs over, the one named last changes fastest.
Arguments:
- tokens: bfloat16 [1024, 384], P(('groups', 'tile'), 'chan'), parts along dimension 0, may hold values from -6 to 6
- conv_a: bfloat16 [27, 384, 384], P(None, 'chan'), may hold values from -0.0625 to 0.0625
- bias_a: float32 [384], P('chan'), may hold values from -3 to 3
- conv_b: bfloat16 [27, 384, 384], P(None, 'chan'), may hold values from -0.0625 to 0.0625
- bias_b: float32 [384], P('chan'), may hold values from -3 to 3
Outputs:
- decoded: bfloat16 [384, 16, 256], P('chan', 'tile', 'groups'), parts along dimension 2
There are 2 independent parts, one for each index of `groups`. A program takes and returns all parts, laid end to end along the dimension named above; an argument that names none is the same for every part. Nothing has to cross between parts.
All inputs are finite; a program needn't handle non-finite values.
Results may differ from a plain program's by a relative error of at most 0.0038.
Values may be sent and summed in bfloat16 or wider, within the bound.
A program may use at most 64 MiB of HBM per device.

v0:
```python
import jax
import jax.numpy as jnp
from jax import lax
from jax.sharding import PartitionSpec as P

TF = 4
H = 16
WD = 2


def extended(x, sides, width):
    for axis, dim in sides:
        peers, length = (lax.axis_size(axis), x.shape[dim])
        up = [(i, (i + 1) % peers) for i in range(peers - 1)]
        down = [(j, i) for i, j in up]
        last = lax.slice_in_dim(x, length - width, length, axis=dim)
        leading = lax.slice_in_dim(x, 0, width, axis=dim)
        before = lax.ppermute(last, axis, up)
        after = lax.ppermute(leading, axis, down)
        x = jnp.concatenate([before, x, after], axis=dim)
    return x


def tap_sum(weight_taps, padded, frames, rows, width):
    total = None
    for frame_step in range(3):
        for row_step in range(3):
            for col_step in range(3):
                tap_index = 9 * frame_step + 3 * row_step + col_step
                view = padded[
                    :,
                    frame_step : frame_step + frames,
                    row_step : row_step + rows,
                    col_step : col_step + width,
                ]
                product = lax.dot_general(
                    weight_taps[tap_index],
                    view,
                    (((0,), (0,)), ((), ())),
                    preferred_element_type=jnp.float32,
                )
                total = product if total is None else total + product
    return total.reshape(total.shape[0], frames * rows * width)


def local_terms(weight, padded, frames, rows, width):
    return tap_sum(weight, padded, frames, rows, width)


def pad_local(field):
    return jnp.pad(field, ((0, 0), (2, 0), (1, 1), (0, 0)))


def local(tokens, conv_a, bias_a, conv_b, bias_b):
    tiles = lax.axis_size("tile")
    local_chan = tokens.shape[1]
    out_rows = conv_a.shape[2] // lax.axis_size("chan")
    block_rows = TF * H // tiles
    sectioned = tokens.reshape(block_rows, tiles, WD * local_chan)
    arrived = lax.all_to_all(sectioned, "tile", split_axis=1, concat_axis=0, tiled=True)
    field = arrived.reshape(TF, H, WD, local_chan).transpose(3, 0, 1, 2)
    wide = extended(field, (("tile", 3),), 1)
    width_a = WD
    pad_a = pad_local(wide)
    sum_a = lax.psum_scatter(
        local_terms(conv_a, pad_a, TF, H, width_a), "chan", scatter_dimension=0, tiled=True
    )
    act_a = jax.nn.silu(sum_a + bias_a[:, None]).reshape(out_rows, TF, H, width_a)
    first = act_a.astype(jnp.bfloat16)
    first_wide = extended(first, (("tile", 3),), 1)
    upsampled = jnp.repeat(jnp.repeat(first_wide, 2, axis=2), 2, axis=3)[:, :, :, 1:-1]
    pad_b = pad_local(upsampled)
    rows_b = 2 * H
    width_b = 2 * WD
    sum_b = lax.psum_scatter(
        local_terms(conv_b, pad_b, TF, rows_b, width_b), "chan", scatter_dimension=0, tiled=True
    )
    decoded = jax.nn.silu(sum_b + bias_b[:, None]).astype(jnp.bfloat16)
    decoded = decoded.reshape(out_rows, TF, rows_b, width_b).transpose(0, 3, 1, 2)
    return decoded.reshape(out_rows, width_b, TF * rows_b)


def solution(mesh):
    in_specs = (
        P(("groups", "tile"), "chan"),
        P(None, "chan", None),
        P("chan"),
        P(None, "chan", None),
        P("chan"),
    )
    out_specs = P("chan", "tile", "groups")
    return jax.shard_map(local, mesh=mesh, in_specs=in_specs, out_specs=out_specs, check_vma=False)
```

profile of v0, /device:TPU:0, one launch (start us, length us, event | category | flops | bytes accessed | tf_op | source)
XLA Modules:
  0.0 106.8 jit_solution(14204958401764551114)
XLA Ops:
  6.5 1.0 copy.14
  7.7 11.8 %all_to_all.15 = bf16[16,4,192]{2,0,1:T(8,128)(2,1)S(1)} all-to-all(bf16[16,4,192]{2,0,1:T(8,128)(2,1)S(1)} %copy.15), channel_id=1, replica_groups=mesh['groups'=2,'tile'=4,'chan'=4] {'tile'}, dimensions={1} | all-to-all | bytes 49152 | tf_op jit(solution)/shard_map/all_to_all | solution.py:60
  19.5 2.6 %collective-permute-start = (bf16[96,4,16,1]{0,2,3,1:T(8,128)(2,1)S(1)}, bf16[96,4,16,1]{0,2,3,1:T(8,128)(2,1)S(1)}, u32[]{:S(2)}, u32[]{:S(2)}) collective-permute-start(bf16[96,4,16,1]{0,2,3,1:T(8,128)(2,1)S(1)} %get-tuple-element.7), channel_id=1, source_target_pairs={{0,4},{4,8},{8,12},{1,5},{5,9},{9,13},{2,6},{6,10},{10,14},{3,7},{... | collective-permute-start | bytes 36872 | tf_op jit(solution)/shard_map/ppermute | solution.py:18
  22.2 1.3 %collective-permute-start.1 = (bf16[96,4,16,1]{0,2,3,1:T(8,128)(2,1)S(1)}, bf16[96,4,16,1]{0,2,3,1:T(8,128)(2,1)S(1)}, u32[]{:S(2)}, u32[]{:S(2)}) collective-permute-start(bf16[96,4,16,1]{0,2,3,1:T(8,128)(2,1)S(1)} %get-tuple-element.8), channel_id=1, source_target_pairs={{4,0},{8,4},{12,8},{5,1},{9,5},{13,9},{6,2},{10,6},{14,10},{7,3},{... | collective-permute-start | bytes 36872 | tf_op jit(solution)/shard_map/ppermute | solution.py:19
  23.5 1.1 fusion.64
  24.6 3.3 %collective-permute-done.1 = bf16[96,4,16,1]{0,2,3,1:T(8,128)(2,1)S(1)} collective-permute-done((bf16[96,4,16,1]{0,2,3,1:T(8,128)(2,1)S(1)}, bf16[96,4,16,1]{0,2,3,1:T(8,128)(2,1)S(1)}, u32[]{:S(2)}, u32[]{:S(2)}) %collective-permute-start.1) | collective-permute-done | bytes 12320 | tf_op jit(solution)/shard_map/ppermute | solution.py:19
  27.9 1.1 convolution_bitcast_fusion.13
  28.9 1.1 convolution_bitcast_fusion.14
  30.0 1.1 convolution_bitcast_fusion.15
  31.0 1.1 convolution_bitcast_fusion.16
  32.8 0.2 convolution_add_fusion.31
  33.1 0.2 convolution_add_fusion.29
  33.5 0.2 convolution_add_fusion.27
  33.7 0.2 convolution_add_fusion.26
  33.8 0.2 convolution_add_fusion.25
  34.0 0.2 convolution_add_fusion.24
  34.2 0.2 convolution_add_fusion.23
  34.4 0.2 convolution_add_fusion.22
  34.6 0.2 convolution_add_fusion.21
  34.9 0.2 convolution_add_fusion.19
  35.1 0.2 convolution_add_fusion.18
  35.4 0.2 fusion.15
  35.6 0.2 fusion.21
  35.8 1.2 %fusion.19 = f32[384,4,16,2]{0,2,3,1:T(8,128)S(1)} fusion(f32[384,4,16,2]{0,2,3,1:T(8,128)S(1)} %convolution_bitcast_fusion.12, f32[384,4,16,2]{0,2,3,1:T(8,128)S(1)} %convolution_bitcast_fusion.13, f32[384,4,16,2]{0,2,3,1:T(8,128)S(1)} %convolution_bitcast_fusion.14, f32[384,4,16,2]{0,2,3,1:T(8,128)S(1)} %fusion.21, bf16[27,96,384]{2,1,0:T(8,128)(2,1)} %param.6, ...), kind=kOutput, calls=%fused_computation.86 | convolution fusion | flops 9707520 | bytes 1093632 | tf_op jit(solution)/shard_map/dot_general | solution.py:36
  37.3 0.8 copy.78
  38.2 18.0 %reduce-scatter.7.cloned.1.call-done = f32[96,128]{1,0:T(8,128)} async-done(((f32[384,128]{1,0:T(8,128)}), f32[96,128]{1,0:T(8,128)}) %reduce-scatter.7.cloned.1.call-update) | async-done | bytes 49168
  56.2 0.9 copy.79
  57.2 3.4 %collective-permute-start.2 = (bf16[96,4,16,1]{0,3,2,1:T(2,128)(2,1)S(1)}, bf16[96,4,16,1]{0,3,2,1:T(2,128)(2,1)S(1)}, u32[]{:S(2)}, u32[]{:S(2)}) collective-permute-start(bf16[96,4,16,1]{0,3,2,1:T(2,128)(2,1)S(1)} %get-tuple-element.5), channel_id=1, source_target_pairs={{0,4},{4,8},{8,12},{1,5},{5,9},{9,13},{2,6},{6,10},{10,14},{3,7},{... | collective-permute-start | bytes 36872 | tf_op jit(solution)/shard_map/ppermute | solution.py:18
  60.6 1.3 %collective-permute-start.3 = (bf16[96,4,16,1]{0,3,2,1:T(2,128)(2,1)S(1)}, bf16[96,4,16,1]{0,3,2,1:T(2,128)(2,1)S(1)}, u32[]{:S(2)}, u32[]{:S(2)}) collective-permute-start(bf16[96,4,16,1]{0,3,2,1:T(2,128)(2,1)S(1)} %get-tuple-element.6), channel_id=1, source_target_pairs={{4,0},{8,4},{12,8},{5,1},{9,5},{13,9},{6,2},{10,6},{14,10},{7,3},{... | collective-permute-start | bytes 36872 | tf_op jit(solution)/shard_map/ppermute | solution.py:19
  61.9 0.3 collective-permute-done.2
  62.2 4.2 %collective-permute-done.3 = bf16[96,4,16,1]{0,3,2,1:T(2,128)(2,1)S(1)} collective-permute-done((bf16[96,4,16,1]{0,3,2,1:T(2,128)(2,1)S(1)}, bf16[96,4,16,1]{0,3,2,1:T(2,128)(2,1)S(1)}, u32[]{:S(2)}, u32[]{:S(2)}) %collective-permute-start.3) | collective-permute-done | bytes 12320 | tf_op jit(solution)/shard_map/ppermute | solution.py:19
  66.7 0.2 convolution_bitcast_fusion.5
  67.0 0.2 convolution_bitcast_fusion.4
  67.2 0.2 convolution_bitcast_fusion.3
  67.4 0.2 fusion.32
  67.7 0.2 convolution_add_fusion.15
  67.9 0.2 convolution_add_fusion.14
  68.2 0.2 convolution_add_fusion.13
  68.4 0.2 convolution_add_fusion.12
  68.7 0.2 convolution_add_fusion.11
  68.9 0.2 convolution_add_fusion.10
  69.2 0.2 convolution_add_fusion.9
  69.4 0.2 convolution_add_fusion.8
  69.7 0.2 convolution_add_fusion.7
  70.0 0.2 convolution_add_fusion.6
  70.2 0.2 convolution_add_fusion.5
  70.5 0.2 convolution_add_fusion.4
  70.7 0.2 convolution_add_fusion.3
  71.0 0.2 convolution_add_fusion.2
  71.2 0.2 convolution_add_fusion.1
  71.5 0.2 fusion.10
  71.7 0.2 fusion.9
  72.0 0.3 fusion.8
  72.2 0.3 fusion.7
  72.5 0.2 fusion.6
  72.7 0.2 fusion.5
  73.0 0.2 fusion.4
  73.2 0.3 fusion.3
  73.5 0.5 copy.19
  74.0 0.3 reshape.34
  74.3 1.1 %copy.80 = f32[384,512]{1,0:T(8,128)} copy(f32[384,512]{0,1:T(8,128)S(1)} %reshape.34) | data formatting | bytes 1572864
  75.5 22.5 %reduce-scatter.9.cloned.1.call-done = f32[96,512]{1,0:T(8,128)} async-done(((f32[384,512]{1,0:T(8,128)}), f32[96,512]{1,0:T(8,128)}) %reduce-scatter.9.cloned.1.call-update) | async-done | bytes 196624
  98.0 1.0 copy.81
  99.1 0.8 copy.21
  (37 shorter events, 2.4 us)
Async XLA Ops:
  6.5 25.6 %copy-start.1 = (bf16[27,96,384]{2,1,0:T(8,128)(2,1)S(1)}, bf16[27,96,384]{2,1,0:T(8,128)(2,1)}, u32[]{:S(2)}) copy-start(bf16[27,96,384]{2,1,0:T(8,128)(2,1)} %param.6) | copy-start | bytes 5971972
  6.5 49.7 %reduce-scatter.7.cloned.1.call-start = ((), (), s32[]{:S(2)}) async-start(), calls=%async_computation.3 | async-start | bytes 245760
  19.5 5.0 %collective-permute-start = (bf16[96,4,16,1]{0,2,3,1:T(8,128)(2,1)S(1)}, bf16[96,4,16,1]{0,2,3,1:T(8,128)(2,1)S(1)}, u32[]{:S(2)}, u32[]{:S(2)}) collective-permute-start(bf16[96,4,16,1]{0,2,3,1:T(8,128)(2,1)S(1)} %get-tuple-element.7), channel_id=1, source_target_pairs={{0,4},{4,8},{8,12},{1,5},{5,9},{9,13},{2,6},{6,10},{10,14},{3,7},{... | collective-permute-start | bytes 36872 | tf_op jit(solution)/shard_map/ppermute | solution.py:18
  22.2 5.6 %collective-permute-start.1 = (bf16[96,4,16,1]{0,2,3,1:T(8,128)(2,1)S(1)}, bf16[96,4,16,1]{0,2,3,1:T(8,128)(2,1)S(1)}, u32[]{:S(2)}, u32[]{:S(2)}) collective-permute-start(bf16[96,4,16,1]{0,2,3,1:T(8,128)(2,1)S(1)} %get-tuple-element.8), channel_id=1, source_target_pairs={{4,0},{8,4},{12,8},{5,1},{9,5},{13,9},{6,2},{10,6},{14,10},{7,3},{... | collective-permute-start | bytes 36872 | tf_op jit(solution)/shard_map/ppermute | solution.py:19
  35.4 21.7 %copy-start.2 = (f32[96]{0:T(128)S(1)}, f32[96]{0:T(128)}, u32[]{:S(2)}) copy-start(f32[96]{0:T(128)} %param.7) | copy-start | bytes 1156
  35.8 30.9 %copy-start = (bf16[27,96,384]{2,1,0:T(8,128)(2,1)S(1)}, bf16[27,96,384]{2,1,0:T(8,128)(2,1)}, u32[]{:S(2)}) copy-start(bf16[27,96,384]{2,1,0:T(8,128)(2,1)} %param.8) | copy-start | bytes 5971972
  38.1 59.9 %reduce-scatter.9.cloned.1.call-start = ((), (), s32[]{:S(2)}) async-start(), calls=%async_computation.4 | async-start | bytes 983040
  57.2 5.0 %collective-permute-start.2 = (bf16[96,4,16,1]{0,3,2,1:T(2,128)(2,1)S(1)}, bf16[96,4,16,1]{0,3,2,1:T(2,128)(2,1)S(1)}, u32[]{:S(2)}, u32[]{:S(2)}) collective-permute-start(bf16[96,4,16,1]{0,3,2,1:T(2,128)(2,1)S(1)} %get-tuple-element.5), channel_id=1, source_target_pairs={{0,4},{4,8},{8,12},{1,5},{5,9},{9,13},{2,6},{6,10},{10,14},{3,7},{... | collective-permute-start | bytes 36872 | tf_op jit(solution)/shard_map/ppermute | solution.py:18
  60.6 5.8 %collective-permute-start.3 = (bf16[96,4,16,1]{0,3,2,1:T(2,128)(2,1)S(1)}, bf16[96,4,16,1]{0,3,2,1:T(2,128)(2,1)S(1)}, u32[]{:S(2)}, u32[]{:S(2)}) collective-permute-start(bf16[96,4,16,1]{0,3,2,1:T(2,128)(2,1)S(1)} %get-tuple-element.6), channel_id=1, source_target_pairs={{4,0},{8,4},{12,8},{5,1},{9,5},{13,9},{6,2},{10,6},{14,10},{7,3},{... | collective-permute-start | bytes 36872 | tf_op jit(solution)/shard_map/ppermute | solution.py:19
  74.0 25.0 %copy-start.3 = (f32[96]{0:T(128)S(1)}, f32[96]{0:T(128)}, u32[]{:S(2)}) copy-start(f32[96]{0:T(128)} %param.9) | copy-start | bytes 1156
Sparse Core Ops, SparseCore 0:
  38.2 17.9 reduce-scatter.6
  75.6 22.3 reduce-scatter.8
where the time goes:
time: 107 us
  waiting for transfers between devices  48.3 us (45%)
  matrix products  16.6 us (16%)
  between operations  14 us (13%)
  blocking collectives  11.8 us (11%)
  starting transfers between devices  8.66 us (8%)
  local copies, waits for them, and re-layouts  7.08 us (7%)
    unnamed x4, waiting for transfers between devices  40.6 us
    dot_general x54, matrix products, tap_sum(): lax.dot_general(weight_taps[tap_index], view, (((0,), (0,)), ((), ())), p...  16.6 us
    all_to_all x1, blocking collectives, local(): lax.all_to_all(sectioned, 'tile', split_axis=1, concat_axis=0, tiled=True)  11.8 us
    ppermute x2, waiting for transfers between devices, extended(): after = lax.ppermute(leading, axis, down)  7.49 us
    ppermute x2, starting transfers between devices, extended(): before = lax.ppermute(last, axis, up)  6.03 us
    unnamed x13, local copies, waits for them, and re-layouts  4.89 us
    ppermute x2, starting transfers between devices, extended(): after = lax.ppermute(leading, axis, down)  2.58 us
  transfers between devices with their start and end apart: 6, of which 5 were waited for; matrix products, arithmetic and copies ran while one was open for 1% of the time, Pallas kernels for 0%

commit v1 on v0

v1 whole, which is shorter than its diff:
```python
import functools

import jax
import jax.numpy as jnp
from jax import lax
from jax.experimental import pallas as pl
from jax.experimental.pallas import tpu as pltpu
from jax.sharding import PartitionSpec as P

TF = 4
H = 16
H2 = 2 * H
WD = 2
LANES = 128
POS = WD * TF * H
COL = TF * H2
MESH = pl.DeviceIdType.MESH
CHUNKS = ((1, 2), (0, 3))


def silu(v):
    return v / (1.0 + jnp.exp(-v))


def kernel(tiles, chans, ch, rows,
           tok_hbm, wa_hbm, ba_hbm, wb_hbm, bb_hbm, out_ref,
           tok, tokf, fsend, frecv, fpad, xs, wa, wb, ba, bb, bias_a,
           asend, arecv, hsend, hrecv, gpad, us, bsend, brecv,
           lsem, fs_sem, fr_sem, as_sem, ar_sem, hs_sem, hr_sem, bs_sem, br_sem):
    mt = lax.axis_index("tile")
    mc = lax.axis_index("chan")
    width = tiles * WD
    f32, bf16 = jnp.float32, jnp.bfloat16

    tok_copy = pltpu.make_async_copy(tok_hbm, tok, lsem.at[0])
    tok_copy.start()
    wa_copy = pltpu.make_async_copy(wa_hbm, wa.at[:, pl.ds(0, ch), :], lsem.at[1])
    wa_copy.start()
    ba_copy = pltpu.make_async_copy(ba_hbm, ba, lsem.at[2])
    ba_copy.start()
    bb_copy = pltpu.make_async_copy(bb_hbm, bb, lsem.at[3])
    bb_copy.start()
    wb_copy = pltpu.make_async_copy(wb_hbm, wb.at[:, pl.ds(0, ch), :], lsem.at[4])
    wb_copy.start()

    hrecv[...] = jnp.zeros_like(hrecv)
    barrier = pltpu.get_barrier_semaphore()
    for k in range(1, tiles):
        pl.semaphore_signal(barrier, inc=1, device_id={"tile": lax.rem(mt + k, tiles)}, device_id_type=MESH)
    for k in range(1, chans):
        pl.semaphore_signal(barrier, inc=1, device_id={"chan": lax.rem(mc + k, chans)}, device_id_type=MESH)

    tokf[...] = jnp.zeros_like(tokf)
    fsend[0] = jnp.zeros_like(fsend[0])
    fsend[width + 1] = jnp.zeros_like(fsend[0])
    tok_copy.wait()
    tokf[:, :ch] = tok[...].astype(f32)
    for w in range(width):
        fsend[w + 1] = tokf[pl.ds(w, rows, stride=width), :].astype(bf16)

    pl.semaphore_wait(barrier, tiles + chans - 2)

    def field_copy(k, src_tile, peer):
        return pltpu.make_async_remote_copy(
            src_ref=fsend.at[pl.ds(WD * peer, WD + 2)], dst_ref=frecv.at[src_tile],
            send_sem=fs_sem.at[k - 1], recv_sem=fr_sem.at[k - 1],
            device_id={"tile": peer}, device_id_type=MESH)

    for k in range(1, tiles):
        field_copy(k, mt, lax.rem(mt + k, tiles)).start()
    frecv[mt] = fsend[pl.ds(WD * mt, WD + 2)]

    wa[:, ch:, :] = jnp.zeros((27, LANES - ch, wa.shape[2]), bf16)
    wb[:, ch:, :] = jnp.zeros((27, LANES - ch, wb.shape[2]), bf16)
    fpad[:, :, 0:8, :] = jnp.zeros((WD + 2, TF, 8, LANES), f32)
    fpad[:, :, 8 + H:16 + H, :] = jnp.zeros((WD + 2, TF, 8, LANES), f32)
    gpad[:, :, 0:8, :] = jnp.zeros((WD + 2, TF, 8, LANES), f32)
    gpad[:, :, 8 + H2:16 + H2, :] = jnp.zeros((WD + 2, TF, 8, LANES), f32)
    xs[:, :, 0:2] = jnp.zeros((3, WD + 2, 2, H, LANES), bf16)
    us[:, :, 0:2] = jnp.zeros((3, WD + 2, 2, H2, LANES), bf16)
    asend[...] = jnp.zeros_like(asend)
    bias_a[...] = jnp.zeros_like(bias_a)
    ba_copy.wait()
    bias_a[:, :ch] = ba[...]

    for k in range(1, tiles):
        field_copy(k, lax.rem(mt + tiles - k, tiles), lax.rem(mt + k, tiles)).wait_recv()

    for s in range(tiles):
        t, h0 = (s * rows) // H, (s * rows) % H
        fpad[:, t, 8 + h0:8 + h0 + rows, :] = frecv[s].astype(f32)
    for e in range(3):
        xs[e, :, 2:] = fpad[:, :, 7 + e:7 + e + H, :].astype(bf16)

    wa_copy.wait()
    lhs = jnp.concatenate(
        [xs[e, g:g + WD, a:a + TF].reshape(POS, LANES)
         for a in range(3) for e in range(3) for g in range(3)], axis=1)
    part = jnp.dot(lhs, wa[...].reshape(27 * LANES, wa.shape[2]), preferred_element_type=f32)
    for j in range(chans):
        asend[j, :, :ch] = part[:, j * ch:(j + 1) * ch]

    def a_copy(k):
        peer = lax.rem(mc + k, chans)
        return pltpu.make_async_remote_copy(
            src_ref=asend.at[peer], dst_ref=arecv.at[k - 1],
            send_sem=as_sem.at[k - 1], recv_sem=ar_sem.at[k - 1],
            device_id={"chan": peer}, device_id_type=MESH)

    for k in range(1, chans):
        a_copy(k).start()
    total = asend[mc] + bias_a[...]
    for k in range(1, chans):
        a_copy(k).wait_recv()
        total = total + arecv[k - 1]
    first = silu(total).astype(bf16).reshape(WD, TF, H, LANES)

    hsend[0] = first[0]
    hsend[1] = first[WD - 1]

    def halo_copy(side, peer):
        return pltpu.make_async_remote_copy(
            src_ref=hsend.at[side], dst_ref=hrecv.at[1 - side],
            send_sem=hs_sem.at[side], recv_sem=hr_sem.at[1 - side],
            device_id={"tile": peer}, device_id_type=MESH)

    has_left = mt > 0
    has_right = mt < tiles - 1

    @pl.when(has_left)
    def _():
        halo_copy(0, mt - 1).start()

    @pl.when(has_right)
    def _():
        halo_copy(1, mt + 1).start()

    def place(w, column):
        column = column.astype(f32)
        for t in range(TF):
            for parity in range(2):
                gpad.at[w, t][pl.ds(8 + parity, H, stride=2), :] = column[t]
        for e in range(3):
            us[e, w, 2:] = gpad[w, :, 7 + e:7 + e + H2, :].astype(bf16)

    for w in range(WD):
        place(w + 1, first[w])

    def b_copy(c, k):
        peer = lax.rem(mc + k, chans)
        return pltpu.make_async_remote_copy(
            src_ref=bsend.at[c, peer], dst_ref=brecv.at[c, k - 1],
            send_sem=bs_sem.at[c, k - 1], recv_sem=br_sem.at[c, k - 1],
            device_id={"chan": peer}, device_id_type=MESH)

    wb_copy.wait()
    bb_copy.wait()
    for c, cols in enumerate(CHUNKS):
        if c == 1:
            @pl.when(has_right)
            def _():
                halo_copy(0, mt).wait_recv()

            @pl.when(has_left)
            def _():
                halo_copy(1, mt).wait_recv()
            place(0, hrecv[0])
            place(WD + 1, hrecv[1])
        lhs = jnp.concatenate(
            [jnp.concatenate(
                [us[e, (w2 + g + 1) // 2, a:a + TF].reshape(COL, LANES) for w2 in cols], axis=0)
             for a in range(3) for e in range(3) for g in range(3)], axis=1)
        part = jnp.dot(lhs, wb[...].reshape(27 * LANES, wb.shape[2]), preferred_element_type=f32)
        for j in range(chans):
            bsend[c, j] = part[:, j * ch:(j + 1) * ch].astype(bf16)
        for k in range(1, chans):
            b_copy(c, k).start()

    for c, cols in enumerate(CHUNKS):
        total = bsend[c, mc].astype(f32) + bb[...]
        for k in range(1, chans):
            b_copy(c, k).wait_recv()
            total = total + brecv[c, k - 1].astype(f32)
        y = silu(total)
        for i, w2 in enumerate(cols):
            out_ref[w2] = y[i * COL:(i + 1) * COL].T.astype(bf16)

    for k in range(1, tiles):
        field_copy(k, mt, lax.rem(mt + k, tiles)).wait_send()
    for k in range(1, chans):
        a_copy(k).wait_send()
        for c in range(2):
            b_copy(c, k).wait_send()

    @pl.when(has_left)
    def _():
        halo_copy(0, mt - 1).wait_send()

    @pl.when(has_right)
    def _():
        halo_copy(1, mt + 1).wait_send()


def local(tokens, conv_a, bias_a, conv_b, bias_b):
    tiles = lax.axis_size("tile")
    chans = lax.axis_size("chan")
    ch = tokens.shape[1]
    rows = TF * H // tiles
    full = conv_a.shape[2]
    width = tiles * WD
    f32, bf16 = jnp.float32, jnp.bfloat16
    vm, dma = pltpu.VMEM, pltpu.SemaphoreType.DMA
    out = pl.pallas_call(
        functools.partial(kernel, tiles, chans, ch, rows),
        out_shape=jax.ShapeDtypeStruct((2 * WD, ch, COL), bf16),
        in_specs=[pl.BlockSpec(memory_space=pl.ANY)] * 5,
        out_specs=pl.BlockSpec(memory_space=vm),
        scratch_shapes=[
            vm((rows * width, ch), bf16),
            vm((rows * width, LANES), f32),
            vm((width + 2, rows, LANES), bf16),
            vm((tiles, WD + 2, rows, LANES), bf16),
            vm((WD + 2, TF, H + 16, LANES), f32),
            vm((3, WD + 2, TF + 2, H, LANES), bf16),
            vm((27, LANES, full), bf16),
            vm((27, LANES, full), bf16),
            vm((1, ch), f32),
            vm((1, ch), f32),
            vm((1, LANES), f32),
            vm((chans, POS, LANES), f32),
            vm((chans - 1, POS, LANES), f32),
            vm((2, TF, H, LANES), bf16),
            vm((2, TF, H, LANES), bf16),
            vm((WD + 2, TF, H2 + 16, LANES), f32),
            vm((3, WD + 2, TF + 2, H2, LANES), bf16),
            vm((2, chans, 2 * COL, ch), bf16),
            vm((2, chans - 1, 2 * COL, ch), bf16),
            dma((5,)),
            dma((tiles - 1,)),
            dma((tiles - 1,)),
            dma((chans - 1,)),
            dma((chans - 1,)),
            dma((2,)),
            dma((2,)),
            dma((2, chans - 1)),
            dma((2, chans - 1)),
        ],
        compiler_params=pltpu.CompilerParams(
            collective_id=0, has_side_effects=True, vmem_limit_bytes=48 << 20),
    )(tokens, conv_a, bias_a.reshape(1, -1), conv_b, bias_b.reshape(1, -1))
    return out.transpose(1, 0, 2)


def solution(mesh):
    in_specs = (
        P(("groups", "tile"), "chan"),
        P(None, "chan", None),
        P("chan"),
        P(None, "chan", None),
        P("chan"),
    )
    out_specs = P("chan", "tile", "groups")
    return jax.shard_map(local, mesh=mesh, in_specs=in_specs, out_specs=out_specs, check_vma=False)
```

time: 107 us -> 27.9 us (0.26)
  the two profiles are of different devices: /device:TPU:0 before, /device:TPU:1 now
where the time goes in v1:
time: 27.9 us; the launch traced here: 27.7 us
  Pallas kernels  21.7 us (78%)
  local copies, waits for them, and re-layouts  5.95 us (21%)
    pallas_call x1, Pallas kernels, local(): pl.pallas_call(functools.partial(kernel, tiles, chans, ch, rows), out_sha...  21.7 us
    unnamed x9, local copies, waits for them, and re-layouts  5.26 us
    transpose x1, local copies, waits for them, and re-layouts, local(): return out.transpose(1, 0, 2)  0.69 us

profile of v1, /device:TPU:1, one launch (start us, length us, event | category | flops | bytes accessed | tf_op | source)
XLA Modules:
  0.0 27.7 jit_solution(7560676248216218874)
XLA Ops:
  0.0 0.8 %copy.6.tok_hbm = bf16[128,96]{1,0:T(8,128)(2,1)S(1)} copy(bf16[128,96]{0,1:T(8,128)(2,1)} %param.5) | data formatting | bytes 49152 | tf_op args[0]
  0.8 0.0 copy-start
  0.9 1.6 %copy-done = bf16[27,96,384]{2,1,0:T(8,128)(2,1)S(1)} copy-done((bf16[27,96,384]{2,1,0:T(8,128)(2,1)S(1)}, bf16[27,96,384]{2,1,0:T(8,128)(2,1)}, u32[]{:S(2)}) %copy-start) | copy-done | bytes 1990680
  2.4 0.0 copy-start.1
  2.4 1.6 %copy-done.1 = bf16[27,96,384]{2,1,0:T(8,128)(2,1)S(1)} copy-done((bf16[27,96,384]{2,1,0:T(8,128)(2,1)S(1)}, bf16[27,96,384]{2,1,0:T(8,128)(2,1)}, u32[]{:S(2)}) %copy-start.1) | copy-done | bytes 1990680
  4.0 0.0 copy-start.2
  4.0 0.7 %copy-done.2 = f32[96]{0:T(128)S(1)} copy-done((f32[96]{0:T(128)S(1)}, f32[96]{0:T(128)}, u32[]{:S(2)}) %copy-start.2) | copy-done | bytes 408
  4.6 0.0 copy-start.3
  4.6 0.7 %copy-done.3 = f32[96]{0:T(128)S(1)} copy-done((f32[96]{0:T(128)S(1)}, f32[96]{0:T(128)}, u32[]{:S(2)}) %copy-start.3) | copy-done | bytes 408
  5.3 21.7 %shard_map.55 = bf16[4,96,128]{2,1,0:T(8,128)(2,1)S(1)} custom-call(bf16[128,96]{1,0:T(8,128)(2,1)S(1)} %copy.6.tok_hbm, bf16[27,96,384]{2,1,0:T(8,128)(2,1)S(1)} %copy-done, f32[1,96]{1,0:T(1,128)S(1)} %bitcast.4, bf16[27,96,384]{2,1,0:T(8,128)(2,1)S(1)} %copy-done.1, f32[1,96]{1,0:T(1,128)S(1)} %bitcast.5), custom_call_target="tpu_custom_call" | custom-call | tf_op jit(solution)/shard_map/pallas_call | solution.py:213
  27.0 0.7 %copy.7 = bf16[96,4,128]{2,1,0:T(4,128)(2,1)} copy(bf16[96,4,128]{2,0,1:T(8,128)(2,1)S(1)} %bitcast.3) | data formatting | bytes 196608 | tf_op jit(solution)/shard_map/transpose | solution.py:251
Async XLA Ops:
  0.8 1.6 %copy-start = (bf16[27,96,384]{2,1,0:T(8,128)(2,1)S(1)}, bf16[27,96,384]{2,1,0:T(8,128)(2,1)}, u32[]{:S(2)}) copy-start(bf16[27,96,384]{2,1,0:T(8,128)(2,1)} %wa_hbm.1) | copy-start | bytes 5971972
  2.4 1.6 %copy-start.1 = (bf16[27,96,384]{2,1,0:T(8,128)(2,1)S(1)}, bf16[27,96,384]{2,1,0:T(8,128)(2,1)}, u32[]{:S(2)}) copy-start(bf16[27,96,384]{2,1,0:T(8,128)(2,1)} %wb_hbm.1) | copy-start | bytes 5971972
  4.0 0.7 %copy-start.2 = (f32[96]{0:T(128)S(1)}, f32[96]{0:T(128)}, u32[]{:S(2)}) copy-start(f32[96]{0:T(128)} %param.7) | copy-start | bytes 1156
  4.6 0.7 %copy-start.3 = (f32[96]{0:T(128)S(1)}, f32[96]{0:T(128)}, u32[]{:S(2)}) copy-start(f32[96]{0:T(128)} %param.9) | copy-start | bytes 1156

commit v2 on v1

--- a/solution.py
+++ b/solution.py
@@ -25,12 +25,16 @@
 def kernel(tiles, chans, ch, rows,
            tok_hbm, wa_hbm, ba_hbm, wb_hbm, bb_hbm, out_ref,
            tok, tokf, fsend, frecv, fpad, xs, wa, wb, ba, bb, bias_a,
-           asend, arecv, hsend, hrecv, gpad, us, bsend, brecv,
-           lsem, fs_sem, fr_sem, as_sem, ar_sem, hs_sem, hr_sem, bs_sem, br_sem):
+           bias_b, asend, a_near, a_pass, a_far, hsend, hrecv, gpad, us, bsend, b_near, b_pass, b_far,
+           lsem, fs_sem, fr_sem, an_sem, am_sem, ap_sem, af_sem, hs_sem, hr_sem,
+           bn_sem, bm_sem, bp_sem, bf_sem):
     mt = lax.axis_index("tile")
     mc = lax.axis_index("chan")
     width = tiles * WD
     f32, bf16 = jnp.float32, jnp.bfloat16
+    pairs = chans // 2
+    side, pair = lax.rem(mc, 2), mc // 2
+    partner = mc + 1 - 2 * side
 
     tok_copy = pltpu.make_async_copy(tok_hbm, tok, lsem.at[0])
     tok_copy.start()
@@ -47,18 +51,20 @@
     barrier = pltpu.get_barrier_semaphore()
     for k in range(1, tiles):
         pl.semaphore_signal(barrier, inc=1, device_id={"tile": lax.rem(mt + k, tiles)}, device_id_type=MESH)
-    for k in range(1, chans):
-        pl.semaphore_signal(barrier, inc=1, device_id={"chan": lax.rem(mc + k, chans)}, device_id_type=MESH)
+    pl.semaphore_signal(barrier, inc=1, device_id={"chan": partner}, device_id_type=MESH)
+    for k in range(1, pairs):
+        pl.semaphore_signal(
+            barrier, inc=1, device_id={"chan": 2 * lax.rem(pair + k, pairs) + side}, device_id_type=MESH)
 
     tokf[...] = jnp.zeros_like(tokf)
     fsend[0] = jnp.zeros_like(fsend[0])
     fsend[width + 1] = jnp.zeros_like(fsend[0])
     tok_copy.wait()
-    tokf[:, :ch] = tok[...].astype(f32)
+    tokf[:, :ch] = tok[...].astype(f32).T
     for w in range(width):
         fsend[w + 1] = tokf[pl.ds(w, rows, stride=width), :].astype(bf16)
 
-    pl.semaphore_wait(barrier, tiles + chans - 2)
+    pl.semaphore_wait(barrier, tiles - 1 + pairs)
 
     def field_copy(k, src_tile, peer):
         return pltpu.make_async_remote_copy(
@@ -78,10 +84,11 @@
     gpad[:, :, 8 + H2:16 + H2, :] = jnp.zeros((WD + 2, TF, 8, LANES), f32)
     xs[:, :, 0:2] = jnp.zeros((3, WD + 2, 2, H, LANES), bf16)
     us[:, :, 0:2] = jnp.zeros((3, WD + 2, 2, H2, LANES), bf16)
-    asend[...] = jnp.zeros_like(asend)
-    bias_a[...] = jnp.zeros_like(bias_a)
     ba_copy.wait()
-    bias_a[:, :ch] = ba[...]
+    bb_copy.wait()
+    for row, column in ((ba, bias_a), (bb, bias_b)):
+        wide = jnp.concatenate([row[...], jnp.zeros((1, LANES - ch), f32)], axis=1)
+        column[...] = jnp.broadcast_to(wide, (LANES, LANES)).T[:ch]
 
     for k in range(1, tiles):
         field_copy(k, lax.rem(mt + tiles - k, tiles), lax.rem(mt + k, tiles)).wait_recv()
@@ -97,23 +104,38 @@
         [xs[e, g:g + WD, a:a + TF].reshape(POS, LANES)
          for a in range(3) for e in range(3) for g in range(3)], axis=1)
     part = jnp.dot(lhs, wa[...].reshape(27 * LANES, wa.shape[2]), preferred_element_type=f32)
+    part = part.T
     for j in range(chans):
-        asend[j, :, :ch] = part[:, j * ch:(j + 1) * ch]
-
-    def a_copy(k):
-        peer = lax.rem(mc + k, chans)
+        asend[j] = part[j * ch:(j + 1) * ch]
+
+    def near_copy(k, send, near, send_sem, recv_sem):
         return pltpu.make_async_remote_copy(
-            src_ref=asend.at[peer], dst_ref=arecv.at[k - 1],
-            send_sem=as_sem.at[k - 1], recv_sem=ar_sem.at[k - 1],
-            device_id={"chan": peer}, device_id_type=MESH)
-
-    for k in range(1, chans):
-        a_copy(k).start()
-    total = asend[mc] + bias_a[...]
-    for k in range(1, chans):
-        a_copy(k).wait_recv()
-        total = total + arecv[k - 1]
-    first = silu(total).astype(bf16).reshape(WD, TF, H, LANES)
+            src_ref=send.at[2 * lax.rem(pair + k, pairs) + 1 - side], dst_ref=near.at[k],
+            send_sem=send_sem.at[k], recv_sem=recv_sem.at[k],
+            device_id={"chan": partner}, device_id_type=MESH)
+
+    def far_copy(k, held, far, send_sem, recv_sem):
+        return pltpu.make_async_remote_copy(
+            src_ref=held.at[k - 1], dst_ref=far.at[k - 1],
+            send_sem=send_sem.at[k - 1], recv_sem=recv_sem.at[k - 1],
+            device_id={"chan": 2 * lax.rem(pair + k, pairs) + side}, device_id_type=MESH)
+
+    order = [*range(1, pairs), 0]
+    a_near_args = (asend, a_near, an_sem, am_sem)
+    a_far_args = (a_pass, a_far, ap_sem, af_sem)
+    for k in order:
+        near_copy(k, *a_near_args).start()
+    for k in range(1, pairs):
+        near_copy(k, *a_near_args).wait_recv()
+        a_pass[k - 1] = asend[2 * lax.rem(pair + k, pairs) + side] + a_near[k]
+        far_copy(k, *a_far_args).start()
+    near_copy(0, *a_near_args).wait_recv()
+    total = asend[mc] + a_near[0] + bias_a[...]
+    for k in range(1, pairs):
+        far_copy(k, *a_far_args).wait_recv()
+        total = total + a_far[k - 1]
+    first = jnp.concatenate([silu(total), jnp.zeros((LANES - ch, POS), f32)], axis=0).T
+    first = first.astype(bf16).reshape(WD, TF, H, LANES)
 
     hsend[0] = first[0]
     hsend[1] = first[WD - 1]
@@ -146,15 +168,13 @@
     for w in range(WD):
         place(w + 1, first[w])
 
-    def b_copy(c, k):
-        peer = lax.rem(mc + k, chans)
-        return pltpu.make_async_remote_copy(
-            src_ref=bsend.at[c, peer], dst_ref=brecv.at[c, k - 1],
-            send_sem=bs_sem.at[c, k - 1], recv_sem=br_sem.at[c, k - 1],
-            device_id={"chan": peer}, device_id_type=MESH)
+    def b_near_args(c):
+        return bsend.at[c], b_near.at[c], bn_sem.at[c], bm_sem.at[c]
+
+    def b_far_args(c):
+        return b_pass.at[c], b_far.at[c], bp_sem.at[c], bf_sem.at[c]
 
     wb_copy.wait()
-    bb_copy.wait()
     for c, cols in enumerate(CHUNKS):
         if c == 1:
             @pl.when(has_right)
@@ -171,26 +191,38 @@
                 [us[e, (w2 + g + 1) // 2, a:a + TF].reshape(COL, LANES) for w2 in cols], axis=0)
              for a in range(3) for e in range(3) for g in range(3)], axis=1)
         part = jnp.dot(lhs, wb[...].reshape(27 * LANES, wb.shape[2]), preferred_element_type=f32)
+        part = part.T.astype(bf16)
         for j in range(chans):
-            bsend[c, j] = part[:, j * ch:(j + 1) * ch].astype(bf16)
-        for k in range(1, chans):
-            b_copy(c, k).start()
-
+            bsend[c, j] = part[j * ch:(j + 1) * ch]
+        for k in order:
+            near_copy(k, *b_near_args(c)).start()
+
+    for c in range(2):
+        for k in range(1, pairs):
+            near_copy(k, *b_near_args(c)).wait_recv()
+            own = bsend[c, 2 * lax.rem(pair + k, pairs) + side].astype(f32)
+            b_pass[c, k - 1] = (own + b_near[c, k].astype(f32)).astype(bf16)
+            far_copy(k, *b_far_args(c)).start()
+
+    bias = jnp.concatenate([bias_b[...]] * 2, axis=1)
     for c, cols in enumerate(CHUNKS):
-        total = bsend[c, mc].astype(f32) + bb[...]
-        for k in range(1, chans):
-            b_copy(c, k).wait_recv()
-            total = total + brecv[c, k - 1].astype(f32)
-        y = silu(total)
+        near_copy(0, *b_near_args(c)).wait_recv()
+        total = bsend[c, mc].astype(f32) + b_near[c, 0].astype(f32) + bias
+        for k in range(1, pairs):
+            far_copy(k, *b_far_args(c)).wait_recv()
+            total = total + b_far[c, k - 1].astype(f32)
+        y = silu(total).astype(bf16)
         for i, w2 in enumerate(cols):
-            out_ref[w2] = y[i * COL:(i + 1) * COL].T.astype(bf16)
+            out_ref[w2] = y[:, i * COL:(i + 1) * COL]
 
     for k in range(1, tiles):
         field_copy(k, mt, lax.rem(mt + k, tiles)).wait_send()
-    for k in range(1, chans):
-        a_copy(k).wait_send()
-        for c in range(2):
-            b_copy(c, k).wait_send()
+    for near_args, far_args in ((a_near_args, a_far_args),
+                                (b_near_args(0), b_far_args(0)), (b_near_args(1), b_far_args(1))):
+        for k in range(pairs):
+            near_copy(k, *near_args).wait_send()
+        for k in range(1, pairs):
+            far_copy(k, *far_args).wait_send()
 
     @pl.when(has_left)
     def _():
@@ -205,6 +237,7 @@
     tiles = lax.axis_size("tile")
     chans = lax.axis_size("chan")
     ch = tokens.shape[1]
+    pairs = chans // 2
     rows = TF * H // tiles
     full = conv_a.shape[2]
     width = tiles * WD
@@ -213,10 +246,10 @@
     out = pl.pallas_call(
         functools.partial(kernel, tiles, chans, ch, rows),
         out_shape=jax.ShapeDtypeStruct((2 * WD, ch, COL), bf16),
-        in_specs=[pl.BlockSpec(memory_space=pl.ANY)] * 5,
+        in_specs=[pl.BlockSpec(memory_space=pltpu.HBM)] * 5,
         out_specs=pl.BlockSpec(memory_space=vm),
         scratch_shapes=[
-            vm((rows * width, ch), bf16),
+            vm((ch, rows * width), bf16),
             vm((rows * width, LANES), f32),
             vm((width + 2, rows, LANES), bf16),
             vm((tiles, WD + 2, rows, LANES), bf16),
@@ -226,28 +259,37 @@
             vm((27, LANES, full), bf16),
             vm((1, ch), f32),
             vm((1, ch), f32),
-            vm((1, LANES), f32),
-            vm((chans, POS, LANES), f32),
-            vm((chans - 1, POS, LANES), f32),
+            vm((ch, LANES), f32),
+            vm((ch, LANES), f32),
+            vm((chans, ch, POS), f32),
+            vm((pairs, ch, POS), f32),
+            vm((pairs - 1, ch, POS), f32),
+            vm((pairs - 1, ch, POS), f32),
             vm((2, TF, H, LANES), bf16),
             vm((2, TF, H, LANES), bf16),
             vm((WD + 2, TF, H2 + 16, LANES), f32),
             vm((3, WD + 2, TF + 2, H2, LANES), bf16),
-            vm((2, chans, 2 * COL, ch), bf16),
-            vm((2, chans - 1, 2 * COL, ch), bf16),
+            vm((2, chans, ch, 2 * COL), bf16),
+            vm((2, pairs, ch, 2 * COL), bf16),
+            vm((2, pairs - 1, ch, 2 * COL), bf16),
+            vm((2, pairs - 1, ch, 2 * COL), bf16),
             dma((5,)),
             dma((tiles - 1,)),
             dma((tiles - 1,)),
-            dma((chans - 1,)),
-            dma((chans - 1,)),
+            dma((pairs,)),
+            dma((pairs,)),
+            dma((pairs - 1,)),
+            dma((pairs - 1,)),
             dma((2,)),
             dma((2,)),
-            dma((2, chans - 1)),
-            dma((2, chans - 1)),
+            dma((2, pairs)),
+            dma((2, pairs)),
+            dma((2, pairs - 1)),
+            dma((2, pairs - 1)),
         ],
         compiler_params=pltpu.CompilerParams(
-            collective_id=0, has_side_effects=True, vmem_limit_bytes=48 << 20),
-    )(tokens, conv_a, bias_a.reshape(1, -1), conv_b, bias_b.reshape(1, -1))
+            collective_id=0, has_side_effects=True, vmem_limit_bytes=63 << 20),
+    )(tokens.T, conv_a, bias_a.reshape(1, -1), conv_b, bias_b.reshape(1, -1))
     return out.transpose(1, 0, 2)
 
 

time: 27.9 us -> 22.8 us (0.82)
  the two profiles are of different devices: /device:TPU:1 before, /device:TPU:0 now
where the time goes in v2:
time: 22.8 us; the launch traced here: 22.7 us
  Pallas kernels  21.1 us (93%)
  local copies, waits for them, and re-layouts  1.58 us (7%)
    pallas_call x1, Pallas kernels, local(): pl.pallas_call(functools.partial(kernel, tiles, chans, ch, rows), out_sha...  21.1 us
    transpose x1, local copies, waits for them, and re-layouts, local(): return out.transpose(1, 0, 2)  1.58 us

profile of v2, /device:TPU:0, one launch (start us, length us, event | category | flops | bytes accessed | tf_op | source)
XLA Modules:
  0.0 22.7 jit_solution(12626219317214707682)
XLA Ops:
  0.0 21.1 %shard_map.55 = bf16[4,96,128]{2,1,0:T(8,128)(2,1)} custom-call(bf16[96,128]{1,0:T(8,128)(2,1)} %bitcast.5, bf16[27,96,384]{2,1,0:T(8,128)(2,1)} %wa_hbm.1, f32[1,96]{1,0:T(1,128)} %bitcast.6, bf16[27,96,384]{2,1,0:T(8,128)(2,1)} %wb_hbm.1, f32[1,96]{1,0:T(1,128)} %bitcast.7), custom_call_target="tpu_custom_call" | custom-call | tf_op jit(solution)/shard_map/pallas_call | solution.py:246
  21.1 1.6 %copy.6 = bf16[96,4,128]{2,1,0:T(4,128)(2,1)} copy(bf16[96,4,128]{2,0,1:T(8,128)(2,1)} %bitcast.4) | data formatting | bytes 196608 | tf_op jit(solution)/shard_map/transpose | solution.py:293
